TPU v7x, 256 devices: a whole 4x4x8 slice. The times are simulated.
256 devices in a mesh: row: 16 (over y_hi, x, core), col: 16 (over y_lo, z).
Axes of the slice: x: 4, y: 4 (y_hi: 2, y_lo: 2; y = y_hi * 2 + y_lo), z: 8, core: 2. Of those that a mesh axis runs over, the one named last changes fastest.
Arguments:
- op_tiles: float32 [512, 16, 64, 64], P('row', 'col'), may hold values from -18 to 18
- op_rows: int32 [512, 16], P('row', 'col'), may hold values from 0 to 7
- op_cols: int32 [512, 16], P('row', 'col'), may hold values from 0 to 7
- op_count: int32 [16, 16], P('row', 'col'), may hold values from 1 to 32, as said below
- pro_tiles: float32 [128, 16, 64, 64], P('row', 'col'), may hold values from -0.125 to 0.125
- pro_cols: int32 [128, 16], P('row', 'col'), may hold values from 0 to 1
- pro_live: int32 [128, 16], P('row', 'col'), may hold values 0 or 1
Outputs:
- product: float32 [128, 32, 64, 64], P('row', 'col')
- coarse: float32 [32, 32, 64, 64], P('row', 'col')
Inputs may be any that keep to these rules, and one draw needn't show every extreme that they name: `op_count`: live slots of each device's list; some device's list is full in every draw.
All inputs are finite; a program needn't handle non-finite values. No bound on the sum of `pro_live` on one device may be relied on, other than what follows from the above.
Results may differ from a plain program's by a relative error of at most 0.0003.
Values sent between devices are 32-bit elements; how exact they have to be, the bound alone decides.
A program may use at most 128 MiB of HBM per device.

v0:
```python
import jax
import jax.numpy as jnp
from jax import lax
from jax.sharding import PartitionSpec as P

COARSEN = 4
precise = lax.Precision.HIGHEST


def broadcast(value, axis, root):
    mine = lax.axis_index(axis) == root
    return lax.psum(jnp.where(mine, value, jnp.zeros_like(value)), axis)


def column_panel(masked_pro, pro_cols):
    return (
        lax.all_gather(masked_pro, "row", axis=0, tiled=True),
        lax.all_gather(pro_cols, "row", axis=0, tiled=True),
    )


def shards(op_tiles, op_rows, op_cols, op_count, pro_tiles, pro_cols, pro_live):
    list_len = op_tiles.shape[0]
    tile_size = op_tiles.shape[2]
    fine_rows = pro_tiles.shape[0]
    row_count = lax.axis_size("row")
    col_count = lax.axis_size("col")
    fine_total = fine_rows * row_count
    fine_cols = fine_total // col_count
    coarse_total = fine_total // COARSEN
    coarse_cols = coarse_total // col_count
    coarse_rows = coarse_total // row_count
    row_index = lax.axis_index("row")
    col_index = lax.axis_index("col")
    live_op = (jnp.arange(list_len, dtype=jnp.int32) < op_count[0, 0]).astype(jnp.float32)
    masked_op = op_tiles[:, 0] * live_op[:, None, None]
    masked_pro = pro_tiles * pro_live.astype(jnp.float32)[:, :, None, None]
    op_where = jnp.stack([op_rows[:, 0], op_cols[:, 0] + col_index * fine_cols], axis=1)
    panel_tiles, panel_ids = column_panel(masked_pro, pro_cols)
    empty_product = jnp.zeros((fine_rows, coarse_cols, tile_size, tile_size), jnp.float32)
    piece_tiles = lax.all_gather(masked_op, "col", axis=0, tiled=True)
    piece_where = lax.all_gather(op_where, "col", axis=0, tiled=True)
    fine_ids = piece_where[:, 1]
    right_tiles = panel_tiles[fine_ids, 0]
    targets = panel_ids[fine_ids, 0]
    tile_prods = jnp.einsum("nab,nbc->nac", piece_tiles, right_tiles, precision=precise)
    product = empty_product.at[piece_where[:, 0], targets].add(tile_prods)
    panel_tiles, panel_ids = column_panel(masked_pro, pro_cols)
    root_col = row_index * coarse_rows // coarse_cols
    far_tiles, far_ids = (
        broadcast(panel_tiles, "col", root_col),
        broadcast(panel_ids, "col", root_col),
    )
    shift_ids = root_col * coarse_cols - row_index * coarse_rows
    empty_owned = jnp.zeros((coarse_rows, coarse_cols, tile_size, tile_size), jnp.float32)
    left_tiles = far_tiles
    left_ids = far_ids + shift_ids
    inside = (left_ids >= 0) & (left_ids < coarse_rows)
    left_tiles = left_tiles * inside.astype(jnp.float32)[:, :, None, None]
    tile_prods = jnp.einsum(
        "ksba,kjbc->ksjac",
        left_tiles,
        lax.all_gather(product, "row", axis=0, tiled=True),
        precision=precise,
    )
    placed = jnp.clip(left_ids, 0, coarse_rows - 1)
    coarse = empty_owned.at[placed.reshape(-1)].add(
        tile_prods.reshape((-1,) + tile_prods.shape[2:])
    )
    return (product, coarse)


def solution(mesh):
    return jax.shard_map(
        shards,
        mesh=mesh,
        in_specs=(
            P("row", "col", None, None),
            P("row", "col"),
            P("row", "col"),
            P("row", "col"),
            P("row", "col", None, None),
            P("row", "col"),
            P("row", "col"),
        ),
        out_specs=(P("row", "col", None, None), P("row", "col", None, None)),
        check_vma=False,
    )
```

profile of v0, /device:TPU:1, one launch (start us, length us, event | category | flops | bytes accessed | tf_op | source)
XLA Modules:
  0.0 547.0 jit_solution(2243945836866424324)
XLA Ops:
  7.2 0.0 copy-start.2
  7.2 0.0 all-gather.7.cloned.1.call-start
  7.2 0.7 convert_bitcast_fusion
  7.9 1.7 broadcast_multiply_fusion
  9.6 0.0 all-gather.7.cloned.1.call-update
  9.6 0.0 all-gather.5.cloned.1.call-start
  10.3 2.3 bitcast_multiply_fusion
  12.7 0.0 all-gather.5.cloned.1.call-update
  12.7 0.0 all-reduce.4.cloned.1.call-start
  12.8 0.7 broadcast_add_fusion
  13.4 0.7 add_bitcast_fusion
  14.1 30.4 %all-gather = s32[16,32,2]{1,2,0:T(2,128)S(1)} all-gather(s32[1,32,2]{1,2,0:T(2,128)S(1)} %add_bitcast_fusion), channel_id=1, replica_groups=mesh['row'=16,'col'=16] {'col'}, dimensions={0}, use_global_device_ids=true | all-gather | bytes 4352 | tf_op jit(solution)/shard_map/all_gather | solution.py:42
  44.5 0.1 reshape.70
  44.6 1.3 dynamic-slice
  46.5 30.3 %all-gather.7.cloned.1.call-done = f32[128,1,64,64]{3,2,1,0:T(8,128)} async-done(((f32[8,1,64,64]{3,2,1,0:T(8,128)}), f32[128,1,64,64]{3,2,1,0:T(8,128)}) %all-gather.7.cloned.1.call-update) | async-done | bytes 2097168 | tf_op jit(solution)/shard_map/all_gather | solution.py:17
  76.8 2.8 broadcast_select_fusion
  79.6 0.0 all-reduce.4.cloned.1.call-update
  79.6 0.0 all-gather.9.cloned.1.call-start
  79.7 0.0 copy-done.2
  79.7 0.1 bitcast_dynamic-update-slice_fusion
  79.8 8.3 %all-reduce.1 = s32[128]{0:T(128)S(1)} all-reduce(s32[128]{0:T(128)S(1)} %bitcast_dynamic-update-slice_fusion), channel_id=1, replica_groups=mesh['row'=16,'col'=16] {'row'}, use_global_device_ids=true, to_apply=%add.1 | all-reduce | flops 128 | bytes 1024
  88.1 3.5 gather_fusion
  91.7 11.7 %gather_fusion.1 = f32[512,64,64]{2,1,0:T(8,128)} fusion(f32[128,1,64,64]{3,2,1,0:T(8,128)} %all-gather.7.cloned.1.call-done, s32[512]{0:T(512)S(1)} %bitcast.41), kind=kCustom, calls=%fused_computation.1 | custom fusion | bytes 16781312 | tf_op jit(solution)/shard_map/gather | solution.py:44
  103.3 158.7 %all-gather.5.cloned.1.call-done = f32[512,64,64]{2,1,0:T(8,128)} async-done(((f32[32,64,64]{2,1,0:T(8,128)}), f32[512,64,64]{2,1,0:T(8,128)}) %all-gather.5.cloned.1.call-update) | async-done | bytes 8388624 | tf_op jit(solution)/shard_map/all_gather | solution.py:41
  262.1 23.9 %fusion.12 = f32[512,64,64]{2,1,0:T(8,128)} fusion(f32[512,64,64]{2,1,0:T(8,128)} %all-gather.5.cloned.1.call-done, f32[512,64,64]{2,1,0:T(8,128)} %gather_fusion.1), kind=kOutput, calls=%fused_computation.31 | convolution fusion | flops 1610612736 | bytes 25165824 | tf_op jit(solution)/shard_map/nab,nbc->nac/dot_general | solution.py:46
  286.0 55.8 %scatter_fusion = f32[8,2,64,64]{3,2,1,0:T(8,128)S(1)} fusion(f32[8,2,64,64]{3,2,1,0:T(8,128)S(1)} %broadcast_in_dim.6, s32[512]{0:T(512)S(1)} %bitcast.42, f32[512,64,64]{2,1,0:T(8,128)} %fusion.12), kind=kCustom, calls=%fused_computation.2 | custom fusion | flops 2097152 | bytes 25169920 | tf_op jit(solution)/shard_map/scatter-add | solution.py:47
  341.8 0.0 copy-start
  341.8 0.8 copy-done
  342.6 0.0 all-gather.9.cloned.1.call-update
  342.6 10.7 %psum.14 = s32[128,1]{0,1:T(1,128)S(1)} all-reduce(s32[128,1]{0,1:T(1,128)S(1)} %broadcast_select_fusion.1), channel_id=1, replica_groups=mesh['row'=16,'col'=16] {'col'}, use_global_device_ids=true, to_apply=%region_1.2 | all-reduce | flops 128 | bytes 1024 | tf_op jit(solution)/shard_map/psum | solution.py:12
  353.3 54.1 %all-reduce.4.cloned.1.call-done = f32[128,1,64,64]{3,2,1,0:T(8,128)} async-done(((f32[128,1,64,64]{3,2,1,0:T(8,128)}), f32[128,1,64,64]{3,2,1,0:T(8,128)}) %all-reduce.4.cloned.1.call-update) | async-done | bytes 2097168 | tf_op jit(solution)/shard_map/psum | solution.py:12
  407.4 87.7 %all-gather.9.cloned.1.call-done = f32[128,2,64,64]{3,2,1,0:T(8,128)} async-done(((f32[8,2,64,64]{3,2,1,0:T(8,128)}), f32[128,2,64,64]{3,2,1,0:T(8,128)}) %all-gather.9.cloned.1.call-update) | async-done | bytes 4194320 | tf_op jit(solution)/shard_map/all_gather | solution.py:63
  495.1 18.5 %fusion.3 = f32[128,2,64,64]{2,3,1,0:T(8,128)} fusion(f32[128,2,64,64]{3,2,1,0:T(8,128)} %all-gather.9.cloned.1.call-done, f32[128,1,64,64]{3,2,1,0:T(8,128)} %all-reduce.4.cloned.1.call-done, f32[128]{0:T(128)S(1)} %fusion.10), kind=kOutput, calls=%fused_computation.7 | convolution fusion | flops 805830656 | bytes 10486272 | tf_op jit(solution)/shard_map/ksba,kjbc->ksjac/dot_general | solution.py:60
  513.6 9.1 %copy.15 = f32[128,2,64,64]{3,2,1,0:T(8,128)} copy(f32[128,2,64,64]{2,3,1,0:T(8,128)} %fusion.3) | data formatting | bytes 8388608 | tf_op jit(solution)/shard_map/reshape | solution.py:68
  522.8 17.0 %scatter_fusion.1 = f32[2,2,64,64]{3,2,1,0:T(8,128)S(1)} fusion(f32[2,2,64,64]{3,2,1,0:T(8,128)S(1)} %broadcast_in_dim.7, s32[128]{0:T(128)S(1)} %fusion.11, f32[128,2,64,64]{3,2,1,0:T(8,128)} %copy.15), kind=kCustom, calls=%fused_computation.3 | custom fusion | flops 1048576 | bytes 12583424 | tf_op jit(solution)/shard_map/scatter-add | solution.py:67
  539.8 0.0 copy-start.1
  539.8 0.6 copy-done.1
  (10 shorter events, 0.1 us)
Async XLA Ops:
  7.2 72.5 %copy-start.2 = (s32[8,1]{0,1:T(1,128)S(1)}, s32[8,1]{0,1:T(1,128)}, u32[]{:S(2)}) copy-start(s32[8,1]{0,1:T(1,128)} %param.12) | copy-start | bytes 100
  7.2 69.6 %all-gather.7.cloned.1.call-start = ((), (), s32[]{:S(2)}) async-start(), calls=%async_computation.1 | async-start | bytes 4456448 | tf_op jit(solution)/shard_map/all_gather | solution.py:17
  9.6 252.4 %all-gather.5.cloned.1.call-start = ((), (), s32[]{:S(2)}) async-start(), calls=%async_computation | async-start | bytes 17825792 | tf_op jit(solution)/shard_map/all_gather | solution.py:41
  12.7 394.7 %all-reduce.4.cloned.1.call-start = ((), (), s32[]{:S(2)}) async-start(), calls=%async_computation.3 | async-start | bytes 8388608 | tf_op jit(solution)/shard_map/psum | solution.py:12
  79.6 415.5 %all-gather.9.cloned.1.call-start = ((), (), s32[]{:S(2)}) async-start(), calls=%async_computation.2 | async-start | bytes 8912896 | tf_op jit(solution)/shard_map/all_gather | solution.py:63
  341.8 0.8 copy-start
  539.8 0.7 copy-start.1
Sparse Core Ops, SparseCore 0:
  11.3 65.4 all-gather.6
  78.6 183.4 all-gather.4
  264.8 142.5 all-reduce.3
  410.5 84.5 all-gather.8
where the time goes:
time: 549 us; the launch traced here: 547 us
  waiting for transfers between devices  331 us (60%)
  other arithmetic  81.6 us (15%)
  blocking collectives  49.4 us (9%)
  matrix products  42.4 us (8%)
  local copies, waits for them, and re-layouts  27.2 us (5%)
  between operations  15.2 us (3%)
    all_gather x1, waiting for transfers between devices, shards(): piece_tiles = lax.all_gather(masked_op, 'col', axis=0, tiled=True)  159 us
    all_gather x1, waiting for transfers between devices, shards(): lax.all_gather(product, 'row', axis=0, tiled=True)  87.7 us
    scatter-add x1, other arithmetic, shards(): product = empty_product.at[piece_where[:, 0], targets].add(tile_prods)  55.8 us
    psum x1, waiting for transfers between devices, broadcast(): return lax.psum(jnp.where(mine, value, jnp.zeros_like(value)), axis)  54.1 us
    all_gather x1, blocking collectives, shards(): piece_where = lax.all_gather(op_where, 'col', axis=0, tiled=True)  30.4 us
    all_gather x1, waiting for transfers between devices, column_panel(): lax.all_gather(masked_pro, 'row', axis=0, tiled=True)  30.3 us
    dot_general x1, matrix products, shards(): jnp.einsum('nab,nbc->nac', piece_tiles, right_tiles, precision=precise)  23.9 us
    dot_general x1, matrix products, shards(): jnp.einsum('ksba,kjbc->ksjac', left_tiles, lax.all_gather(product, 'row',...  18.5 us
  transfers between devices with their start and end apart: 4, of which 4 were waited for; matrix products, arithmetic and copies ran while one was open for 19% of the time, Pallas kernels for 0%

commit v1 on v0

--- a/solution.py
+++ b/solution.py
@@ -60,7 +60,9 @@
     tile_prods = jnp.einsum(
         "ksba,kjbc->ksjac",
         left_tiles,
-        lax.all_gather(product, "row", axis=0, tiled=True),
+        jnp.concatenate(
+            lax.all_to_all(jnp.stack([product] * lax.axis_size("row")), "row", 0, 0), axis=0
+        ),
         precision=precise,
     )
     placed = jnp.clip(left_ids, 0, coarse_rows - 1)

time: 549 us -> 587 us (1.069)
  the two profiles are of different devices: /device:TPU:1 before, /device:TPU:2 now
where the time goes in v1:
time: 587 us; the launch traced here: 585 us
  waiting for transfers between devices  247 us (42%)
  blocking collectives  131 us (22%)
  other arithmetic  95.2 us (16%)
  local copies, waits for them, and re-layouts  52.1 us (9%)
  matrix products  36.5 us (6%)
  between operations  15.2 us (3%)
  starting transfers between devices  7.1 us (1%)
    all_gather x1, waiting for transfers between devices, shards(): piece_tiles = lax.all_gather(masked_op, 'col', axis=0, tiled=True)  174 us
    psum x1, blocking collectives, broadcast(): return lax.psum(jnp.where(mine, value, jnp.zeros_like(value)), axis)  82.1 us
    psum x1, waiting for transfers between devices, broadcast(): return lax.psum(jnp.where(mine, value, jnp.zeros_like(value)), axis)  65.4 us
    scatter-add x1, other arithmetic, shards(): product = empty_product.at[piece_where[:, 0], targets].add(tile_prods)  55.6 us
    all_gather x1, blocking collectives, shards(): piece_where = lax.all_gather(op_where, 'col', axis=0, tiled=True)  36.4 us
    unnamed x11, local copies, waits for them, and re-layouts  27.2 us
    dot_general x1, matrix products, shards(): jnp.einsum('nab,nbc->nac', piece_tiles, right_tiles, precision=precise)  23.8 us
    scatter-add x1, other arithmetic, shards(): empty_owned.at[placed.reshape(-1)]  17 us
  transfers between devices with their start and end apart: 4, of which 4 were waited for; matrix products, arithmetic and copies ran while one was open for 8% of the time, Pallas kernels for 0%

profile of v1, /device:TPU:2, one launch (start us, length us, event | category | flops | bytes accessed | tf_op | source)
XLA Modules:
  0.0 584.7 jit_solution(10219009736339331927)
XLA Ops:
  7.2 0.0 all-gather.6.cloned.1.call-start
  7.2 0.7 convert_bitcast_fusion
  7.9 1.7 broadcast_multiply_fusion
  9.6 0.0 all-gather.6.cloned.1.call-update
  9.6 0.0 all-gather.4.cloned.1.call-start
  10.3 2.3 bitcast_multiply_fusion
  12.7 0.0 all-gather.4.cloned.1.call-update
  12.7 0.7 broadcast_add_fusion
  13.4 0.7 add_bitcast_fusion
  14.0 36.4 %all-gather = s32[16,32,2]{1,2,0:T(2,128)S(1)} all-gather(s32[1,32,2]{1,2,0:T(2,128)S(1)} %add_bitcast_fusion), channel_id=1, replica_groups=mesh['row'=16,'col'=16] {'col'}, dimensions={0}, use_global_device_ids=true | all-gather | bytes 4352 | tf_op jit(solution)/shard_map/all_gather | solution.py:42
  50.5 0.1 reshape.76
  50.6 1.3 dynamic-slice
  52.5 0.8 bitcast_dynamic-update-slice_fusion
  53.3 12.6 %all-reduce.1 = s32[128]{0:T(128)S(1)} all-reduce(s32[128]{0:T(128)S(1)} %bitcast_dynamic-update-slice_fusion), channel_id=1, replica_groups=mesh['row'=16,'col'=16] {'row'}, use_global_device_ids=true, to_apply=%add.1 | all-reduce | flops 128 | bytes 1024
  65.8 3.5 gather_fusion
  69.4 6.0 %all-gather.6.cloned.1.call-done = f32[128,1,64,64]{3,2,1,0:T(8,128)} async-done(((f32[8,1,64,64]{3,2,1,0:T(8,128)}), f32[128,1,64,64]{3,2,1,0:T(8,128)}) %all-gather.6.cloned.1.call-update) | async-done | bytes 2097168 | tf_op jit(solution)/shard_map/all_gather | solution.py:17
  75.4 11.7 %gather_fusion.1 = f32[512,64,64]{2,1,0:T(8,128)} fusion(f32[128,1,64,64]{3,2,1,0:T(8,128)} %all-gather.6.cloned.1.call-done, s32[512]{0:T(512)S(1)} %bitcast.45), kind=kCustom, calls=%fused_computation.1 | custom fusion | bytes 16781312 | tf_op jit(solution)/shard_map/gather | solution.py:44
  87.0 174.5 %all-gather.4.cloned.1.call-done = f32[512,64,64]{2,1,0:T(8,128)} async-done(((f32[32,64,64]{2,1,0:T(8,128)}), f32[512,64,64]{2,1,0:T(8,128)}) %all-gather.4.cloned.1.call-update) | async-done | bytes 8388624 | tf_op jit(solution)/shard_map/all_gather | solution.py:41
  261.5 23.8 %fusion.12 = f32[512,64,64]{2,1,0:T(8,128)} fusion(f32[512,64,64]{2,1,0:T(8,128)} %all-gather.4.cloned.1.call-done, f32[512,64,64]{2,1,0:T(8,128)} %gather_fusion.1), kind=kOutput, calls=%fused_computation.32 | convolution fusion | flops 1610612736 | bytes 25165824 | tf_op jit(solution)/shard_map/nab,nbc->nac/dot_general | solution.py:46
  285.3 55.6 %scatter_fusion = f32[8,2,64,64]{3,2,1,0:T(8,128)S(1)} fusion(f32[8,2,64,64]{3,2,1,0:T(8,128)S(1)} %broadcast_in_dim.6, s32[512]{0:T(512)S(1)} %bitcast.46, f32[512,64,64]{2,1,0:T(8,128)} %fusion.12), kind=kCustom, calls=%fused_computation.2 | custom fusion | flops 2097152 | bytes 25169920 | tf_op jit(solution)/shard_map/scatter-add | solution.py:47
  340.9 0.0 copy-start
  340.9 0.2 copy.14
  341.1 4.3 broadcast_bitcast_fusion
  345.4 13.3 %reshape.80 = f32[16,1,65536]{2,1,0:T(1,128)} reshape(f32[16,8,2,64,64]{4,3,2,1,0:T(8,128)} %broadcast_bitcast_fusion) | data formatting | bytes 8388608
  358.7 0.0 copy-done
  358.7 7.0 %all-to-all-start = ((f32[16,1,65536]{2,1,0:T(1,128)}), f32[16,1,65536]{2,1,0:T(1,128)}, u32[]{:S(2)}, u32[]{:S(2)}) async-start(f32[16,1,65536]{2,1,0:T(1,128)} %reshape.80), calls=%async_computation | async-start | bytes 8388608 | tf_op jit(solution)/shard_map/all_to_all | solution.py:64
  365.7 0.0 all-reduce.4.cloned.1.call-start
  365.7 2.8 broadcast_select_fusion
  368.5 0.0 all-reduce.4.cloned.1.call-update
  368.6 82.1 %psum.14 = s32[128,1]{0,1:T(1,128)S(1)} all-reduce(s32[128,1]{0,1:T(1,128)S(1)} %broadcast_select_fusion.1), channel_id=1, replica_groups=mesh['row'=16,'col'=16] {'col'}, use_global_device_ids=true, to_apply=%region_1.2 | all-reduce | flops 128 | bytes 1024 | tf_op jit(solution)/shard_map/psum | solution.py:12
  450.8 1.4 all-to-all-done
  452.2 0.5 broadcast.109
  452.7 13.7 %reduce = f32[16,65536]{1,0:T(8,128)} reduce(f32[16,1,65536]{2,1,0:T(1,128)} %all-to-all-done, f32[]{:T(128)} %broadcast.109), dimensions={1}, to_apply=%all_to_all.3.reduce_sub_computation | reduce | bytes 8388612 | tf_op jit(solution)/shard_map/all_to_all | solution.py:64
  466.4 6.9 %reshape.81 = f32[16,8,2,64,64]{4,3,2,1,0:T(8,128)} reshape(f32[16,65536]{1,0:T(8,128)} %reduce) | data formatting | bytes 8388608
  473.3 65.4 %all-reduce.4.cloned.1.call-done = f32[128,1,64,64]{3,2,1,0:T(8,128)} async-done(((f32[128,1,64,64]{3,2,1,0:T(8,128)}), f32[128,1,64,64]{3,2,1,0:T(8,128)}) %all-reduce.4.cloned.1.call-update) | async-done | bytes 2097168 | tf_op jit(solution)/shard_map/psum | solution.py:12
  538.7 12.8 %fusion.3 = f32[128,2,64,64]{2,3,1,0:T(8,128)} fusion(f32[128,2,64,64]{2,3,1,0:T(8,128)} %bitcast.47, f32[128,1,64,64]{3,2,1,0:T(8,128)} %all-reduce.4.cloned.1.call-done, f32[128]{0:T(128)S(1)} %fusion.10), kind=kOutput, calls=%fused_computation.7 | convolution fusion | flops 805830656 | bytes 10486272 | tf_op jit(solution)/shard_map/ksba,kjbc->ksjac/dot_general | solution.py:60
  551.5 9.0 %copy.15 = f32[128,2,64,64]{3,2,1,0:T(8,128)} copy(f32[128,2,64,64]{2,3,1,0:T(8,128)} %fusion.3) | data formatting | bytes 8388608 | tf_op jit(solution)/shard_map/reshape | solution.py:70
  560.5 17.0 %scatter_fusion.1 = f32[2,2,64,64]{3,2,1,0:T(8,128)S(1)} fusion(f32[2,2,64,64]{3,2,1,0:T(8,128)S(1)} %broadcast_in_dim.7, s32[128]{0:T(128)S(1)} %fusion.11, f32[128,2,64,64]{3,2,1,0:T(8,128)} %copy.15), kind=kCustom, calls=%fused_computation.3 | custom fusion | flops 1048576 | bytes 12583424 | tf_op jit(solution)/shard_map/scatter-add | solution.py:69
  577.5 0.0 copy-start.1
  577.5 0.6 copy-done.1
  (10 shorter events, 0.1 us)
Async XLA Ops:
  7.2 68.2 %all-gather.6.cloned.1.call-start = ((), (), s32[]{:S(2)}) async-start(), calls=%async_computation.2 | async-start | bytes 4456448 | tf_op jit(solution)/shard_map/all_gather | solution.py:17
  9.6 251.9 %all-gather.4.cloned.1.call-start = ((), (), s32[]{:S(2)}) async-start(), calls=%async_computation.1 | async-start | bytes 17825792 | tf_op jit(solution)/shard_map/all_gather | solution.py:41
  340.9 17.8 %copy-start = (f32[8,2,64,64]{3,2,1,0:T(8,128)}, f32[8,2,64,64]{3,2,1,0:T(8,128)S(1)}, u32[]{:S(2)}) copy-start(f32[8,2,64,64]{3,2,1,0:T(8,128)S(1)} %scatter_fusion) | copy-start | bytes 786436
  358.7 93.5 %all-to-all-start = ((f32[16,1,65536]{2,1,0:T(1,128)}), f32[16,1,65536]{2,1,0:T(1,128)}, u32[]{:S(2)}, u32[]{:S(2)}) async-start(f32[16,1,65536]{2,1,0:T(1,128)} %reshape.80), calls=%async_computation | async-start | bytes 8388608 | tf_op jit(solution)/shard_map/all_to_all | solution.py:64
  365.7 173.0 %all-reduce.4.cloned.1.call-start = ((), (), s32[]{:S(2)}) async-start(), calls=%async_computation.3 | async-start | bytes 8388608 | tf_op jit(solution)/shard_map/psum | solution.py:12
  577.5 0.7 copy-start.1
Sparse Core Ops, SparseCore 0:
  11.3 64.0 all-gather.5
  77.1 184.3 all-gather.3
  369.1 169.5 all-reduce.3
